TPU v7x, 128 devices: a whole 4x4x4 slice. The times are simulated.
128 devices in a mesh: section: 8 (over z_hi, y), seq: 8 (over x, z_lo), mp: 2 (over core).
Axes of the slice: x: 4, y: 4, z: 4 (z_hi: 2, z_lo: 2; z = z_hi * 2 + z_lo), core: 2. Of those that a mesh axis runs over, the one named last changes fastest.
Arguments:
- resid: bfloat16 [8, 2048, 4096], P('section', 'seq', 'mp'), may hold values from -3 to 3
- span_q: bfloat16 [8, 2048, 4096], P('section', 'seq', 'mp'), may hold values from -6 to 6
- span_k: bfloat16 [8, 2048, 4096], P('section', 'seq', 'mp'), may hold values from -6 to 6
- span_v: bfloat16 [8, 2048, 4096], P('section', 'seq', 'mp'), may hold values from -6 to 6
- cache_k: bfloat16 [4, 2048, 4096], P(None, 'seq', 'mp'), may hold values from -6 to 6
- cache_v: bfloat16 [4, 2048, 4096], P(None, 'seq', 'mp'), may hold values from -6 to 6
- cache_index: int32 [8], P('section'), may hold values from 0 to 3
- tile_mask: int32 [8, 16, 48], P('section'), may hold values from 0 to 1, as said below
Outputs:
- updated: bfloat16 [8, 2048, 4096], P('section', 'seq', 'mp')
Inputs may be any that keep to these rules, and one draw needn't show every extreme that they name: tile_mask[s, i, i] is 1 for every group s and query tile i: every query tile sees its own key tile.
All inputs are finite; a program needn't handle non-finite values.
Results may differ from a plain program's by a relative error of at most 0.0044.
Values may be sent and summed in bfloat16 or wider, within the bound.
A program may use at most 320 MiB of HBM per device.

v0:
```python
import math

import jax
import jax.numpy as jnp
from jax import lax
from jax.sharding import PartitionSpec as P

HD = 128
TILE = 128


def shifted(value, axis, steps):
    count = lax.axis_size(axis)
    first, last = (max(0, -steps), min(count, count - steps))
    return lax.ppermute(value, axis, [(source, source + steps) for source in range(first, last)])


def spread(block, axis, holder):
    block = jnp.where(lax.axis_index(axis) == holder, block, jnp.zeros_like(block))
    return lax.psum(block, axis)


def one_hot_rows(ids, count):
    return (ids[:, None] == jnp.arange(count)[None, :]).astype(jnp.float32)


def absorb(carry, queries, keys, values, allowed):
    top, total, acc = carry
    count = keys.shape[0]
    heads = queries.shape[1]
    key_heads = keys.reshape(count, heads, HD)
    value_heads = values.reshape(count, heads, HD)
    score = jnp.einsum("qhd,khd->hqk", queries, key_heads, preferred_element_type=jnp.float32) * (
        1.0 / math.sqrt(HD)
    )
    masked = jnp.where(allowed[None], score, -1e30)
    new_top = jnp.maximum(top, jnp.max(masked, axis=2))
    expo = jnp.where(allowed[None], jnp.exp(masked - new_top[:, :, None]), 0.0)
    factor = jnp.exp(top - new_top)
    total = total * factor + jnp.sum(expo, axis=2)
    mixed = jnp.einsum(
        "hqk,khd->qhd", expo.astype(jnp.bfloat16), value_heads, preferred_element_type=jnp.float32
    )
    acc = acc * factor.T[:, :, None] + mixed
    return (new_top, total, acc)


def body(resid, span_q, span_k, span_v, cache_k, cache_v, cache_index, tile_mask):
    incoming = shifted(resid, "section", 1)
    rows = span_q.shape[1]
    width = span_q.shape[2]
    heads = width // HD
    final_section = lax.axis_size("section") - 1
    query_tiles = tile_mask.shape[1]
    key_tiles = tile_mask.shape[2]
    mask_rows = tile_mask[0].astype(jnp.float32)
    cached_k = lax.dynamic_index_in_dim(cache_k, cache_index[0], 0, keepdims=False)
    cached_v = lax.dynamic_index_in_dim(cache_v, cache_index[0], 0, keepdims=False)
    fresh_k, fresh_v = (
        spread(span_k[0], "section", final_section),
        spread(span_v[0], "section", final_section),
    )
    first_row = lax.axis_index("seq") * rows
    query_ids = (first_row + jnp.arange(rows)) // TILE
    row_allow = jnp.dot(one_hot_rows(query_ids, query_tiles), mask_rows)
    queries = span_q[0].reshape(rows, heads, HD)
    init = (
        jnp.full((heads, rows), -1e30, jnp.float32),
        jnp.zeros((heads, rows), jnp.float32),
        jnp.zeros((rows, heads, HD), jnp.float32),
    )
    carry = init
    pieces = (
        lax.all_gather(span_k[0], "seq", axis=0, tiled=True),
        lax.all_gather(span_v[0], "seq", axis=0, tiled=True),
        lax.all_gather(fresh_k, "seq", axis=0, tiled=True),
        lax.all_gather(fresh_v, "seq", axis=0, tiled=True),
        lax.all_gather(cached_k, "seq", axis=0, tiled=True),
        lax.all_gather(cached_v, "seq", axis=0, tiled=True),
    )
    count = pieces[0].shape[0]
    for group in range(3):
        tiles = jnp.arange(count) // TILE + group * query_tiles
        allowed = jnp.dot(row_allow, one_hot_rows(tiles, key_tiles).T) > 0.5
        carry = absorb(carry, queries, pieces[2 * group], pieces[2 * group + 1], allowed)
    top, total, acc = carry
    attn = (acc / total.T[:, :, None]).reshape(rows, width).astype(jnp.bfloat16)
    attn = lax.optimization_barrier(attn)
    updated = (incoming[0].astype(jnp.float32) + attn.astype(jnp.float32)).astype(jnp.bfloat16)
    return updated[None]


def solution(mesh):
    placed = (
        P("section", "seq", "mp"),
        P("section", "seq", "mp"),
        P("section", "seq", "mp"),
        P("section", "seq", "mp"),
        P(None, "seq", "mp"),
        P(None, "seq", "mp"),
        P("section"),
        P("section", None, None),
    )
    return jax.shard_map(
        body, mesh=mesh, in_specs=placed, out_specs=P("section", "seq", "mp"), check_vma=False
    )
```

profile of v0, /device:TPU:0, one launch (start us, length us, event | category | flops | bytes accessed | tf_op | source)
XLA Modules:
  0.0 1183.3 jit_solution(3314172403509252847)
XLA Ops:
  7.4 0.0 all-reduce.3.cloned.1.call-start
  7.4 1.5 copy.18
  8.9 1.9 copy.26
  10.7 1.1 select_bitcast_fusion.1
  11.8 1.1 select_bitcast_fusion
  12.9 0.0 all-reduce.3.cloned.1.call-update
  12.9 0.0 all-gather.21.cloned.1.call-start
  13.6 2.3 constant_dynamic-slice_fusion
  15.9 0.0 all-gather.21.cloned.1.call-update
  15.9 0.0 all-gather.17.cloned.1.call-start
  16.0 0.5 all-gather.17.cloned.1.call-update
  16.5 0.0 all-gather.19.cloned.1.call-start
  16.6 1.3 constant_dynamic-slice_fusion.1
  17.9 1.3 copy.38
  19.2 0.0 all-gather.19.cloned.1.call-update
  19.2 0.0 all-gather.15.cloned.1.call-start
  19.3 0.7 all-gather.15.cloned.1.call-update
  19.9 0.0 all-gather.11.cloned.1.call-start
  20.0 101.9 %all-reduce.3.cloned.1.call-done = (bf16[256,2048]{0,1:T(8,128)(2,1)}, bf16[256,2048]{0,1:T(8,128)(2,1)}) async-done(((bf16[256,2048]{0,1:T(8,128)(2,1)}, bf16[256,2048]{0,1:T(8,128)(2,1)}), (bf16[256,2048]{0,1:T(8,128)(2,1)}, bf16[256,2048]{0,1:T(8,128)(2,1)})) %all-reduce.3.cloned.1.call-update) | async-done | bytes 2097168 | tf_op jit(solution)/shard_map/psum | solution.py:20
  121.9 0.0 all-gather.11.cloned.1.call-update
  121.9 0.0 all-gather.13.cloned.1.call-start
  122.0 2.3 collective-permute-start
  124.3 0.0 all-gather.13.cloned.1.call-update
  124.3 1.5 copy.39
  125.8 0.9 fusion.35
  126.7 1.0 convolution_compare_fusion
  127.7 1.0 convolution_compare_fusion.1
  128.6 1.0 convolution_compare_fusion.2
  129.6 118.6 %all-gather.21.cloned.1.call-done = bf16[1,2048,2048]{2,1,0:T(8,128)(2,1)} async-done(((bf16[1,256,2048]{2,1,0:T(8,128)(2,1)}), bf16[1,2048,2048]{2,1,0:T(8,128)(2,1)}) %all-gather.21.cloned.1.call-update) | async-done | bytes 8388624 | tf_op jit(solution)/shard_map/all_gather | solution.py:79
  248.2 12.3 %copy.31 = bf16[1,2048,2048]{1,2,0:T(8,128)(2,1)} copy(bf16[1,2048,2048]{2,1,0:T(8,128)(2,1)} %all-gather.21.cloned.1.call-done) | data formatting | bytes 16777216 | tf_op jit(solution)/shard_map/all_gather | solution.py:79
  260.5 158.1 %all-gather.17.cloned.1.call-done = bf16[1,2048,2048]{2,1,0:T(8,128)(2,1)} async-done(((bf16[1,256,2048]{2,1,0:T(8,128)(2,1)}), bf16[1,2048,2048]{2,1,0:T(8,128)(2,1)}) %all-gather.17.cloned.1.call-update) | async-done | bytes 8388624 | tf_op jit(solution)/shard_map/all_gather | solution.py:75
  418.6 12.3 %copy.21 = bf16[1,2048,2048]{1,2,0:T(8,128)(2,1)} copy(bf16[1,2048,2048]{2,1,0:T(8,128)(2,1)} %all-gather.17.cloned.1.call-done) | data formatting | bytes 16777216 | tf_op jit(solution)/shard_map/all_gather | solution.py:75
  431.0 161.4 %all-gather.19.cloned.1.call-done = bf16[1,2048,2048]{1,2,0:T(8,128)(2,1)} async-done(((bf16[1,256,2048]{1,2,0:T(8,128)(2,1)}), bf16[1,2048,2048]{1,2,0:T(8,128)(2,1)}) %all-gather.19.cloned.1.call-update) | async-done | bytes 8388624 | tf_op jit(solution)/shard_map/all_gather | solution.py:78
  592.3 18.6 %fusion.2 = (f32[16,256]{1,0:T(8,128)S(1)}, f32[16,2048,256]{1,2,0:T(8,128)}) fusion(pred[256,2048]{1,0:T(8,128)(4,1)S(1)} %convolution_compare_fusion, bf16[2048,16,128]{0,2,1:T(8,128)(2,1)} %bitcast.123, bf16[256,16,128]{2,1,0:T(8,128)(2,1)S(1)} %bitcast.120), kind=kOutput, calls=%fused_computation.8 | convolution fusion | flops 2172645376 | bytes 43532288 | tf_op jit(solution)/shard_map/qhd,khd->hqk/dot_general | solution.py:33
  610.9 153.9 %all-gather.15.cloned.1.call-done = bf16[1,2048,2048]{1,2,0:T(8,128)(2,1)} async-done(((bf16[1,256,2048]{1,2,0:T(8,128)(2,1)}), bf16[1,2048,2048]{1,2,0:T(8,128)(2,1)}) %all-gather.15.cloned.1.call-update) | async-done | bytes 8388624 | tf_op jit(solution)/shard_map/all_gather | solution.py:74
  764.7 18.5 %fusion = (f32[16,256]{1,0:T(8,128)S(1)}, f32[16,256,2048]{2,1,0:T(8,128)}) fusion(pred[256,2048]{1,0:T(8,128)(4,1)S(1)} %convolution_compare_fusion.2, bf16[2048,16,128]{0,2,1:T(8,128)(2,1)} %bitcast.124, bf16[256,16,128]{2,1,0:T(8,128)(2,1)S(1)} %bitcast.121), kind=kOutput, calls=%fused_computation.6 | convolution fusion | flops 2172645376 | bytes 43532288 | tf_op jit(solution)/shard_map/qhd,khd->hqk/dot_general | solution.py:33
  783.3 153.9 %all-gather.11.cloned.1.call-done = bf16[2048,2048]{0,1:T(8,128)(2,1)} async-done(((bf16[256,2048]{0,1:T(8,128)(2,1)}), bf16[2048,2048]{0,1:T(8,128)(2,1)}) %all-gather.11.cloned.1.call-update) | async-done | bytes 8388624 | tf_op jit(solution)/shard_map/all_gather | solution.py:76
  937.2 18.6 %fusion.1 = (f32[16,256]{1,0:T(8,128)S(1)}, f32[16,2048,256]{1,2,0:T(8,128)}) fusion(pred[256,2048]{1,0:T(8,128)(4,1)S(1)} %convolution_compare_fusion.1, bf16[2048,16,128]{0,2,1:T(8,128)(2,1)} %bitcast.125, bf16[256,16,128]{2,1,0:T(8,128)(2,1)S(1)} %bitcast.122), kind=kOutput, calls=%fused_computation.7 | convolution fusion | flops 2172645376 | bytes 43532288 | tf_op jit(solution)/shard_map/qhd,khd->hqk/dot_general | solution.py:33
  955.8 0.0 slice-start.1
  955.8 17.0 %fusion.7 = f32[16,256]{1,0:T(8,128)S(1)} fusion(f32[16,2048,256]{1,2,0:T(8,128)} %get-tuple-element.15, f32[16,256]{1,0:T(8,128)S(1)} %get-tuple-element.9, pred[256,2048]{1,0:T(8,128)(4,1)S(1)} %convolution_compare_fusion), kind=kLoop, calls=%fused_computation.13 | loop fusion | flops 41938944 | bytes 34111488 | tf_op jit(solution)/shard_map/reduce_sum | solution.py:40
  972.8 15.7 %fusion.9 = f32[16,128,256]{2,1,0:T(8,128)} fusion(bf16[2048,16,128]{0,2,1:T(8,128)(2,1)S(1)} %bitcast.129, f32[16,2048,256]{1,2,0:T(8,128)} %get-tuple-element.15, f32[16,256]{1,0:T(8,128)S(1)} %get-tuple-element.9, pred[256,2048]{1,0:T(8,128)(4,1)S(1)} %convolution_compare_fusion), kind=kOutput, calls=%fused_computation.15 | convolution fusion | flops 2189426688 | bytes 44580864 | tf_op jit(solution)/shard_map/hqk,khd->qhd/dot_general | solution.py:41
  988.4 121.2 %all-gather.13.cloned.1.call-done = bf16[2048,2048]{0,1:T(8,128)(2,1)} async-done(((bf16[256,2048]{0,1:T(8,128)(2,1)}), bf16[2048,2048]{0,1:T(8,128)(2,1)}) %all-gather.13.cloned.1.call-update) | async-done | bytes 8388624 | tf_op jit(solution)/shard_map/all_gather | solution.py:77
  1109.6 18.2 %fusion.11 = f32[16,128,256]{2,1,0:T(8,128)} fusion(bf16[2048,16,128]{0,2,1:T(8,128)(2,1)} %bitcast.132, f32[16,2048,256]{1,2,0:T(8,128)} %get-tuple-element.17, f32[16,256]{1,0:T(8,128)S(1)} %get-tuple-element.10, pred[256,2048]{1,0:T(8,128)(4,1)S(1)} %convolution_compare_fusion.1), kind=kOutput, calls=%fused_computation.16 | convolution fusion | flops 2189426688 | bytes 44580864 | tf_op jit(solution)/shard_map/hqk,khd->qhd/dot_general | solution.py:41
  1127.9 26.2 %fusion.3 = (f32[16,256]{1,0:T(8,128)S(1)}, f32[16,256]{1,0:T(8,128)S(1)}) fusion(f32[16,256,2048]{2,1,0:T(8,128)} %get-tuple-element.19, f32[16,256]{1,0:T(8,128)S(1)} %get-tuple-element.13, pred[256,2048]{1,0:T(8,128)(4,1)S(1)} %convolution_compare_fusion.2, f32[16,256]{1,0:T(8,128)S(1)} %get-tuple-element.10, f32[16,2048,256]{1,2,0:T(8,128)} %get-tuple-element.17, ...), kind=kLoop, calls=%fused_computation.9 | loop fusion | flops 83877888 | bytes 68222976 | tf_op jit(solution)/shard_map/reduce_sum | solution.py:40
  1154.1 18.6 %fusion.20 = bf16[256,16,128]{0,2,1:T(8,128)(2,1)S(1)} fusion(f32[16,128,256]{2,1,0:T(8,128)} %fusion.9, f32[16,128,256]{2,1,0:T(8,128)} %fusion.11, bf16[2048,16,128]{0,2,1:T(8,128)(2,1)} %bitcast.126, f32[16,256,2048]{2,1,0:T(8,128)} %get-tuple-element.19, f32[16,256]{1,0:T(8,128)S(1)} %get-tuple-element.13, ...), kind=kOutput, calls=%fused_computation.28 | convolution fusion | flops 2193096704 | bytes 47792128 | tf_op jit(solution)/shard_map/hqk,khd->qhd/dot_general | solution.py:41
  1172.6 0.6 copy.32
  1173.3 0.0 collective-permute-done
  1173.3 2.6 fusion.25
  (12 shorter events, 0.1 us)
Async XLA Ops:
  7.4 114.5 %all-reduce.3.cloned.1.call-start = ((), (), s32[]{:S(2)}) async-start(), calls=%async_computation.6 | async-start | bytes 4194304 | tf_op jit(solution)/shard_map/psum | solution.py:20
  8.9 10.4 copy-start
  12.9 235.3 %all-gather.21.cloned.1.call-start = ((), (), s32[]{:S(2)}) async-start(), calls=%async_computation.5 | async-start | bytes 9437184 | tf_op jit(solution)/shard_map/all_gather | solution.py:79
  15.9 402.7 %all-gather.17.cloned.1.call-start = ((), (), s32[]{:S(2)}) async-start(), calls=%async_computation.3 | async-start | bytes 9437184 | tf_op jit(solution)/shard_map/all_gather | solution.py:75
  16.5 575.8 %all-gather.19.cloned.1.call-start = ((), (), s32[]{:S(2)}) async-start(), calls=%async_computation.4 | async-start | bytes 9437184 | tf_op jit(solution)/shard_map/all_gather | solution.py:78
  19.2 745.5 %all-gather.15.cloned.1.call-start = ((), (), s32[]{:S(2)}) async-start(), calls=%async_computation.2 | async-start | bytes 9437184 | tf_op jit(solution)/shard_map/all_gather | solution.py:74
  19.9 917.2 %all-gather.11.cloned.1.call-start = ((), (), s32[]{:S(2)}) async-start(), calls=%async_computation | async-start | bytes 9437184 | tf_op jit(solution)/shard_map/all_gather | solution.py:76
  121.9 987.7 %all-gather.13.cloned.1.call-start = ((), (), s32[]{:S(2)}) async-start(), calls=%async_computation.1 | async-start | bytes 9437184 | tf_op jit(solution)/shard_map/all_gather | solution.py:77
  122.0 1051.3 %collective-permute-start = (bf16[1,256,2048]{2,1,0:T(8,128)(2,1)}, bf16[1,256,2048]{2,1,0:T(8,128)(2,1)}, u32[]{:S(2)}, u32[]{:S(2)}) collective-permute-start(bf16[1,256,2048]{2,1,0:T(8,128)(2,1)} %param.8), channel_id=1, source_target_pairs={{0,16},{16,32},{32,48},{48,64},{64,80},{80,96},{96,112},{1,17},{17... | collective-permute-start | bytes 3145736 | tf_op jit(solution)/shard_map/ppermute | solution.py:15
  955.7 17.0 %slice-start = ((s8[8388608]{0:T(1024)(128)(4,1)}), s8[4194304]{0:T(1024)(128)(4,1)S(1)}, s32[]{:S(2)}) async-start(s8[8388608]{0:T(1024)(128)(4,1)} %bitcast.127), calls=%async_computation.7 | async-start | bytes 8388608
  955.8 17.0 %slice-start.1 = ((s8[8388608]{0:T(1024)(128)(4,1)}), s8[4194304]{0:T(1024)(128)(4,1)S(1)}, s32[]{:S(2)}) async-start(s8[8388608]{0:T(1024)(128)(4,1)} %bitcast.127), calls=%async_computation.8 | async-start | bytes 8388608
Sparse Core Ops, SparseCore 0:
  13.0 108.8 all-reduce.2
Sparse Core Ops, SparseCore 1:
  16.0 232.1 all-gather.20
  249.7 168.9 all-gather.16
  420.1 172.2 all-gather.18
  593.9 170.8 all-gather.14
  766.3 170.8 all-gather.10
  938.8 170.8 all-gather.12
where the time goes:
time: 1190 us; the launch traced here: 1180 us
  waiting for transfers between devices  970 us (82%)
  matrix products  112 us (9%)
  other arithmetic  47.9 us (4%)
  local copies, waits for them, and re-layouts  35 us (3%)
  between operations  15.7 us (1%)
    all_gather x1, waiting for transfers between devices, body(): lax.all_gather(cached_k, 'seq', axis=0, tiled=True)  161 us
    all_gather x1, waiting for transfers between devices, body(): lax.all_gather(span_v[0], 'seq', axis=0, tiled=True)  158 us
    all_gather x1, waiting for transfers between devices, body(): lax.all_gather(fresh_k, 'seq', axis=0, tiled=True)  154 us
    all_gather x1, waiting for transfers between devices, body(): lax.all_gather(span_k[0], 'seq', axis=0, tiled=True)  154 us
    all_gather x1, waiting for transfers between devices, body(): lax.all_gather(fresh_v, 'seq', axis=0, tiled=True)  121 us
    all_gather x1, waiting for transfers between devices, body(): lax.all_gather(cached_v, 'seq', axis=0, tiled=True)  119 us
    psum x1, waiting for transfers between devices, spread(): return lax.psum(block, axis)  102 us
    dot_general x3, matrix products, absorb(): jnp.einsum('qhd,khd->hqk', queries, key_heads, preferred_element_type=jnp...  55.6 us
  transfers between devices with their start and end apart: 8, of which 7 were waited for; matrix products, arithmetic and copies ran while one was open for 16% of the time, Pallas kernels for 0%

commit v1 on v0

v1 whole, which is shorter than its diff:
```python
import functools
import math

import jax
import jax.numpy as jnp
from jax import lax
from jax.experimental import pallas as pl
from jax.experimental.pallas import tpu as pltpu
from jax.sharding import PartitionSpec as P

HD = 128
TILE = 128
MESH = pl.DeviceIdType.MESH
HBM = pl.BlockSpec(memory_space=pl.ANY)
VMEM = pl.BlockSpec(memory_space=pltpu.VMEM)
F32 = jnp.float32
BF16 = jnp.bfloat16
RATE = math.log2(math.e) / math.sqrt(HD)
OTHERS = ((2, 1), (1, 1), (3, 1), (2, 0), (0, 1), (1, 0), (3, 0))


def place():
    section, seq = lax.axis_index("section"), lax.axis_index("seq")
    return section // 4, lax.rem(section, 4), seq // 2, lax.rem(seq, 2)


def device(hi, y, x, lo):
    return {"section": hi * 4 + y, "seq": x * 2 + lo}


def head_slice(hi, x, lo):
    return 2 * x + lo + (1 - hi) * (1 - 2 * lo)


def other(step):
    hi, y, x, lo = place()
    return hi, y, lax.rem(x + step[0], 4), lax.rem(lo + step[1], 2)


TREES = (
    {7: ("up",), 4: ("up", "cross"), 5: ("up",), 0: ("up", "down"), 3: ("down",)},
    {7: ("down", "cross"), 6: ("down", "cross"), 3: ("up",), 5: ("down", "cross")},
)
PIECES = 4
LOW = -1e30
Q, K, V, CK, CV = range(5)


def fused_kernel(
    span, q, k, v, ck, cv, resid, bias, attn, inc,
    qb, kb, vb, ob, score_a, score_b, top, total, acc,
    sends, arrivals, shifts, fresh, relay_sends, out_sends, out_arrivals,
):
    hi, y, x, lo = place()
    section, seq = lax.axis_index("section"), lax.axis_index("seq")
    rows, block, part_rows = span // 8, span // 2, span // PIECES
    near = {
        "up": device(hi, lax.rem(y + 1, 4), x, lo),
        "down": device(hi, lax.rem(y + 3, 4), x, lo),
        "cross": device(1 - hi, y, x, 1 - lo),
    }
    following = {"section": lax.rem(section + 1, 8)}
    barrier = pltpu.get_barrier_semaphore()
    greeted = [device(*other(step)) for step in OTHERS] + list(near.values())
    greeted += [following, {"section": lax.rem(section + 7, 8)}]
    for target in greeted:
        pl.semaphore_signal(barrier, inc=1, device_id=target, device_id_type=MESH)
    pl.semaphore_wait(barrier, len(greeted))

    mine = head_slice(hi, x, lo)
    source = {Q: q, K: k, V: v, CK: ck, CV: cv}
    home = {Q: (qb, 0), K: (kb, 0), V: (vb, 0), CK: (kb, 2 * span), CV: (vb, 2 * span)}

    def columns(which, head):
        return pl.ds(pl.multiple_of(which * 2 * HD + head * HD, HD), HD)

    def spread(part, head):
        buffer, first = home[part]
        landing = buffer.at[head, pl.ds(pl.multiple_of(first + seq * rows, rows), rows)]
        piece = seq // (8 // PIECES)
        for step in OTHERS:
            there = other(step)
            pltpu.make_async_remote_copy(
                src_ref=source[part].at[:, columns(head_slice(there[0], there[2], there[3]), head)],
                dst_ref=landing,
                send_sem=sends.at[part, head],
                recv_sem=arrivals.at[part, head, piece],
                device_id=device(*there),
                device_id_type=MESH,
            ).start()
        pltpu.make_async_copy(
            source[part].at[:, columns(mine, head)], landing, arrivals.at[part, head, piece]
        ).start()

    def shift():
        return pltpu.make_async_remote_copy(
            src_ref=resid,
            dst_ref=inc,
            send_sem=shifts.at[0],
            recv_sem=shifts.at[1],
            device_id=following,
            device_id_type=MESH,
        )

    is_last = section == 7

    @pl.when(is_last)
    def _():
        for part, head in ((K, 0), (V, 0), (K, 1), (V, 1), (Q, 0), (CK, 0), (CV, 0), (Q, 1), (CK, 1), (CV, 1)):
            spread(part, head)

    @pl.when(jnp.logical_not(is_last))
    def _():
        for head in range(2):
            for part in (K, V, Q, CK, CV):
                spread(part, head)

    @pl.when(jnp.logical_and(section < 7, section != 3))
    def _():
        shift().start()

    top[...] = jnp.full_like(top, LOW / 2)
    total[...] = jnp.zeros_like(total)
    acc[...] = jnp.zeros_like(acc)

    def settle(ref, sem):
        pltpu.make_async_copy(ref, ref, sem).wait()

    def arrived(part, head, piece):
        buffer, first = home[part]
        settle(buffer.at[head, pl.ds(first + piece * part_rows, part_rows)], arrivals.at[part, head, piece])

    def all_arrived(part, head):
        for piece in range(PIECES):
            arrived(part, head, piece)

    def stream(tree):
        return kb if tree == 0 else vb

    def fresh_arrived(tree, head, piece):
        block_ref = stream(tree).at[head, pl.ds(span + piece * part_rows, part_rows)]
        settle(block_ref, fresh.at[tree, head, piece])

    def pass_on(tree, head, piece, first, slot, target):
        return pltpu.make_async_remote_copy(
            src_ref=stream(tree).at[head, pl.ds(first + piece * part_rows, part_rows)],
            dst_ref=stream(tree).at[head, pl.ds(span + piece * part_rows, part_rows)],
            send_sem=relay_sends.at[tree, head, piece, slot],
            recv_sem=fresh.at[tree, head, piece],
            device_id=near[target],
            device_id_type=MESH,
        )

    def relay(tree, head, piece):
        for node, targets in TREES[tree].items():
            if node == 7:
                continue

            @pl.when(section == node)
            def _():
                fresh_arrived(tree, head, piece)
                for slot, target in enumerate(targets):
                    pass_on(tree, head, piece, span, slot, target).start()

    def leaf(tree):
        inner = [section != node for node in TREES[tree]]
        return functools.reduce(jnp.logical_and, inner)

    def take_fresh(tree, head, pieces):
        @pl.when(leaf(tree))
        def _():
            for piece in pieces:
                fresh_arrived(tree, head, piece)

    @pl.when(is_last)
    def _():
        for head in range(2):
            for tree, part in ((0, K), (1, V)):
                for piece in range(PIECES):
                    arrived(part, head, piece)
                    for slot, target in enumerate(TREES[tree][7]):
                        pass_on(tree, head, piece, 0, slot, target).start()
        all_arrived(Q, 0)

    @pl.when(jnp.logical_not(is_last))
    def _():
        for piece in range(PIECES):
            relay(0, 0, piece)
        all_arrived(K, 0)
        all_arrived(Q, 0)

    def do(action, *args):
        return functools.partial(action, *args)

    others = {
        (0, 0): [do(all_arrived, V, 0), do(relay, 1, 0, 0)],
        (0, 1): [do(relay, 1, 0, 1)],
        (1, 0): [do(relay, 1, 0, 2)],
        (1, 1): [do(relay, 1, 0, 3)] + [do(relay, 0, 1, p) for p in range(4)] + [do(all_arrived, CK, 0)],
        (2, 0): [do(all_arrived, CV, 0), do(relay, 1, 1, 0)],
        (2, 1): [do(relay, 1, 1, 1)],
        (3, 0): [do(relay, 1, 1, 2)],
        (3, 1): [do(relay, 1, 1, 3), do(take_fresh, 0, 0, (0, 1))],
        (4, 0): [do(take_fresh, 1, 0, (0, 1))],
        (4, 1): [do(take_fresh, 0, 0, (2, 3))],
        (5, 0): [do(take_fresh, 1, 0, (2, 3))],
        (5, 1): [do(all_arrived, Q, 1), do(all_arrived, K, 1)],
        (6, 0): [do(all_arrived, V, 1)],
        (7, 1): [do(take_fresh, 0, 1, (0, 1))],
        (8, 0): [do(take_fresh, 1, 1, (0, 1))],
        (8, 1): [do(take_fresh, 0, 1, (2, 3))],
        (9, 0): [do(take_fresh, 1, 1, (2, 3))],
        (9, 1): [do(all_arrived, CK, 1)],
        (10, 0): [do(all_arrived, CV, 1)],
    }
    last = {
        (3, 1): [do(all_arrived, CK, 0)],
        (4, 0): [do(all_arrived, CV, 0)],
        (5, 1): [do(all_arrived, Q, 1)],
        (9, 1): [do(all_arrived, CK, 1)],
        (10, 0): [do(all_arrived, CV, 1)],
    }

    def point(stage, at):
        for wanted, table in ((is_last, last), (jnp.logical_not(is_last), others)):
            for (number, where), actions in table.items():
                if where == at:

                    @pl.when(jnp.logical_and(stage == number, wanted))
                    def _():
                        for action in actions:
                            action()

    tiles = block // TILE

    def locate(stage):
        head, step = stage // 6, lax.rem(stage, 6)
        move = jnp.where(step < 2, 0, jnp.where(step < 4, 2, -2))
        index = step + jnp.where(jnp.logical_or(is_last, head == 1), 0, move)
        fresh_block = jnp.logical_and(index >= 2, index < 4)
        stored = index - jnp.where(jnp.logical_and(is_last, fresh_block), 2, 0)
        return head, index, pl.ds(pl.multiple_of(stored * block, block), block)

    def half_rows(half):
        return pl.ds(pl.multiple_of(half * block, block), block)

    def score(stage, half, out):
        head, _, keys = locate(stage)
        out[...] = lax.dot_general(
            kb[head, keys, :],
            qb[head, half_rows(half), :],
            (((1,), (1,)), ((), ())),
            preferred_element_type=F32,
        )

    def absorb(stage, half, scores):
        head, index, keys = locate(stage)
        biases = [
            jnp.concatenate(
                [jnp.full((1, TILE), bias[half * tiles + u, index * tiles + t], F32) for u in range(tiles)],
                axis=1,
            )
            for t in range(tiles)
        ]
        old = top[head, half]
        new = old
        for t in range(tiles):
            new = jnp.maximum(new, jnp.max(scores[pl.ds(t * TILE, TILE), :], axis=0, keepdims=True) + biases[t])
        top[head, half] = new
        factor = jnp.exp2((old - new) * RATE)
        expo = [
            jnp.exp2((scores[pl.ds(t * TILE, TILE), :] - (new - biases[t])) * RATE) for t in range(tiles)
        ]
        summed = total[head, half] * factor
        for part in expo:
            summed = summed + jnp.sum(part, axis=0, keepdims=True)
        total[head, half] = summed
        weight = jnp.concatenate([part.astype(BF16) for part in expo], axis=0)
        acc[head, half] = acc[head, half] * factor + lax.dot_general(
            vb[head, keys, :], weight, (((0,), (0,)), ((), ())), preferred_element_type=F32
        )

    def result(head):
        return attn.at[:, columns(mine, head)]

    def finish(head, half):
        ob[head, half_rows(half), :] = (acc[head, half] / total[head, half]).T.astype(BF16)
        for step in OTHERS:
            there = other(step)

            @pl.when(there[2] // 2 == half)
            def _():
                owner = there[2] * 2 + there[3]
                pltpu.make_async_remote_copy(
                    src_ref=ob.at[head, pl.ds(pl.multiple_of(owner * rows, rows), rows)],
                    dst_ref=result(head),
                    send_sem=out_sends.at[head],
                    recv_sem=out_arrivals.at[head],
                    device_id=device(*there),
                    device_id_type=MESH,
                ).start()

        @pl.when(x // 2 == half)
        def _():
            pltpu.make_async_copy(
                ob.at[head, pl.ds(pl.multiple_of(seq * rows, rows), rows)], result(head), out_arrivals.at[head]
            ).start()

    far = 1 - x // 2
    score(0, far, score_a)

    def stage_body(stage, carry):
        head, ends = stage // 6, lax.rem(stage, 6) == 5
        point(stage, 0)

        @pl.when(jnp.logical_and(stage == 6, section == 3))
        def _():
            shift().start()

        score(stage, 1 - far, score_b)
        absorb(stage, far, score_a)

        @pl.when(ends)
        def _():
            finish(head, far)

        point(stage, 1)
        score(jnp.minimum(stage + 1, 11), far, score_a)
        absorb(stage, 1 - far, score_b)

        @pl.when(ends)
        def _():
            finish(head, 1 - far)

        return carry

    lax.fori_loop(0, 12, stage_body, 0)

    for tree in range(2):
        for node, targets in TREES[tree].items():

            @pl.when(section == node)
            def _():
                for head in range(2):
                    for piece in range(PIECES):
                        for slot, target in enumerate(targets):
                            pass_on(tree, head, piece, span, slot, target).wait_send()

    @pl.when(section < 7)
    def _():
        shift().wait_send()

    @pl.when(section > 0)
    def _():
        shift().wait_recv()

    for head in range(2):
        for part in range(5):
            settle(home[part][0].at[head, pl.ds(0, 7 * rows)], sends.at[part, head])
        settle(ob.at[head, pl.ds(0, 7 * rows)], out_sends.at[head])
        settle(ob.at[head], out_arrivals.at[head])


def fused(q, k, v, ck, cv, resid, bias):
    rows, width = q.shape
    span = rows * 8
    half = span // 2
    dma = pltpu.SemaphoreType.DMA
    return pl.pallas_call(
        functools.partial(fused_kernel, span),
        out_shape=(jax.ShapeDtypeStruct((rows, width), BF16), jax.ShapeDtypeStruct((rows, width), BF16)),
        in_specs=[HBM] * 6 + [pl.BlockSpec(memory_space=pltpu.SMEM)],
        out_specs=[HBM] * 2,
        scratch_shapes=[
            pltpu.VMEM((2, span, HD), BF16),
            pltpu.VMEM((2, 3 * span, HD), BF16),
            pltpu.VMEM((2, 3 * span, HD), BF16),
            pltpu.VMEM((2, span, HD), BF16),
            pltpu.VMEM((half, half), F32),
            pltpu.VMEM((half, half), F32),
            pltpu.VMEM((2, 2, 1, half), F32),
            pltpu.VMEM((2, 2, 1, half), F32),
            pltpu.VMEM((2, 2, HD, half), F32),
            dma((5, 2)),
            dma((5, 2, PIECES)),
            dma((2,)),
            dma((2, 2, PIECES)),
            dma((2, 2, PIECES, 2)),
            dma((2,)),
            dma((2,)),
        ],
        name="fused",
        compiler_params=pltpu.CompilerParams(
            collective_id=0, has_side_effects=True, vmem_limit_bytes=60 * 2**20
        ),
    )(q, k, v, ck, cv, resid, bias)


def body(resid, span_q, span_k, span_v, cache_k, cache_v, cache_index, tile_mask):
    cached_k = lax.dynamic_index_in_dim(cache_k, cache_index[0], 0, keepdims=False)
    cached_v = lax.dynamic_index_in_dim(cache_v, cache_index[0], 0, keepdims=False)
    bias = jnp.where(tile_mask[0] > 0, 0.0, LOW).astype(F32)
    attn, incoming = fused(span_q[0], span_k[0], span_v[0], cached_k, cached_v, resid[0], bias)
    incoming = jnp.where(lax.axis_index("section") == 0, jnp.zeros_like(incoming), incoming)
    return (incoming.astype(F32) + attn.astype(F32)).astype(BF16)[None]


def solution(mesh):
    placed = (
        P("section", "seq", "mp"),
        P("section", "seq", "mp"),
        P("section", "seq", "mp"),
        P("section", "seq", "mp"),
        P(None, "seq", "mp"),
        P(None, "seq", "mp"),
        P("section"),
        P("section", None, None),
    )
    return jax.shard_map(
        body, mesh=mesh, in_specs=placed, out_specs=P("section", "seq", "mp"), check_vma=False
    )
```

time: 1190 us -> 116 us (0.10)
  waiting for transfers between devices: 970 us -> 0 us
  matrix products: 112 us -> 0 us
  Pallas kernels: 0 us -> 109 us
  other arithmetic: 47.9 us -> 3.19 us
  local copies, waits for them, and re-layouts: 35 us -> 3.12 us
  between operations: 15.7 us -> 0.69 us
    all_gather x6 -> x0, waiting for transfers between devices: 867 us -> none  [the longest x1 161 us: body(): lax.all_gather(cached_k, 'seq', axis=0, tiled=True)]
    dot_general x10 -> x0, matrix products: 112 us -> none  [the longest x3 55.6 us: absorb(): jnp.einsum('qhd,khd->hqk', queries, key_heads, preferred_element_type=jnp...]
    pallas_call x0 -> x1, Pallas kernels: none -> 109 us  [fused(): pl.pallas_call(functools.partial(fused_kernel, span), out_shape=(jax.Shap...]
    psum x1 -> x0, waiting for transfers between devices: 102 us -> none  [spread(): return lax.psum(block, axis)]
    reduce_sum x2 -> x0, other arithmetic: 43.1 us -> none  [absorb(): total = total * factor + jnp.sum(expo, axis=2)]
    all_gather x2 -> x0, local copies, waits for them, and re-layouts: 24.7 us -> none  [the longest x1 12.3 us: body(): lax.all_gather(span_v[0], 'seq', axis=0, tiled=True)]
  transfers between devices with their start and end apart: 8 -> 0, of which waited for: 7 -> 0; matrix products, arithmetic and copies ran while one was open for 16% -> 0% of each run, Pallas kernels for 0% -> 0%
where the time goes in v1:
time: 116 us
  Pallas kernels  109 us (94%)
  other arithmetic  3.19 us (3%)
  local copies, waits for them, and re-layouts  3.12 us (3%)
    pallas_call x1, Pallas kernels, fused(): pl.pallas_call(functools.partial(fused_kernel, span), out_shape=(jax.Shap...  109 us
    squeeze x1, local copies, waits for them, and re-layouts, body(): lax.dynamic_index_in_dim(cache_v, cache_index[0], 0, keepdims=False)  3.11 us
    broadcast_in_dim x1, other arithmetic, body(): return (incoming.astype(F32) + attn.astype(F32)).astype(BF16)[None]  2.59 us

profile of v1, /device:TPU:0, one launch (start us, length us, event | category | flops | bytes accessed | tf_op | source)
XLA Modules:
  0.0 115.6 jit_solution(18260938547148442614)
XLA Ops:
  0.0 0.0 copy-start
  0.7 3.1 %dynamic-slice_bitcast_fusion = (bf16[256,2048]{1,0:T(8,128)(2,1)}, bf16[256,2048]{1,0:T(8,128)(2,1)}) fusion(bf16[4,256,2048]{2,1,0:T(8,128)(2,1)} %param.13, s32[]{:T(128)S(6)} %select_n.20, bf16[4,256,2048]{2,1,0:T(8,128)(2,1)} %param.12), kind=kLoop, calls=%fused_computation.2 | loop fusion | bytes 4194308 | tf_op jit(solution)/shard_map/jit(dynamic_index_in_dim)/squeeze | solution.py:401
  3.8 0.0 copy-done
  3.8 0.6 select_bitcast_fusion.bias
  4.4 108.6 %fused.1 = (bf16[256,2048]{1,0:T(8,128)(2,1)}, bf16[256,2048]{1,0:T(8,128)(2,1)}) custom-call(bf16[256,2048]{1,0:T(8,128)(2,1)} %bitcast.16, bf16[256,2048]{1,0:T(8,128)(2,1)} %bitcast.17, bf16[256,2048]{1,0:T(8,128)(2,1)} %bitcast.18, bf16[256,2048]{1,0:T(8,128)(2,1)} %get-tuple-element.10.ck, bf16[256,2048]{1,0:T(8,128)(2,1)} %get-tuple-element.9.cv, ...), custom_call_target="tpu_custom_call" | custom-call | tf_op jit(solution)/shard_map/fused/pallas_call | solution.py:369
  113.0 2.6 %fusion = bf16[1,256,2048]{2,1,0:T(8,128)(2,1)} fusion(bf16[256,2048]{1,0:T(8,128)(2,1)} %get-tuple-element.8, bf16[256,2048]{1,0:T(8,128)(2,1)} %get-tuple-element.7, pred[]{:T(512)S(6)} %eq.3), kind=kLoop, calls=%fused_computation.1 | loop fusion | flops 2621440 | bytes 3145729 | tf_op jit(solution)/shard_map/broadcast_in_dim | solution.py:405
Async XLA Ops:
  0.0 3.8 %copy-start = (s32[1,16,48]{2,1,0:T(8,128)S(1)}, s32[1,16,48]{2,1,0:T(8,128)}, u32[]{:S(2)}) copy-start(s32[1,16,48]{2,1,0:T(8,128)} %param.15) | copy-start | bytes 9220

commit v2 on v1

--- a/solution.py
+++ b/solution.py
@@ -42,14 +42,15 @@
     {7: ("down", "cross"), 6: ("down", "cross"), 3: ("up",), 5: ("down", "cross")},
 )
 PIECES = 4
+NEARER = (4, 5, 0)
 LOW = -1e30
 Q, K, V, CK, CV = range(5)
 
 
 def fused_kernel(
-    span, q, k, v, ck, cv, resid, bias, attn, inc,
-    qb, kb, vb, ob, score_a, score_b, top, total, acc,
-    sends, arrivals, shifts, fresh, relay_sends, out_sends, out_arrivals,
+    span, q, k, v, cache_k, cache_v, resid, chosen, mask, out,
+    qb, kb, vb, ob, score_a, score_b, top, total, acc, bias, all_ck, all_cv, ck, cv, attn, inc, via,
+    sends, arrivals, shifts, fresh, relay_sends, out_sends, out_arrivals, loads, detours,
 ):
     hi, y, x, lo = place()
     section, seq = lax.axis_index("section"), lax.axis_index("seq")
@@ -60,12 +61,28 @@
         "cross": device(1 - hi, y, x, 1 - lo),
     }
     following = {"section": lax.rem(section + 1, 8)}
+    caches = [
+        pltpu.make_async_copy(whole, held, loads.at[i])
+        for i, (whole, held) in enumerate(((cache_k, all_ck), (cache_v, all_cv)))
+    ]
+    for copy in caches:
+        copy.start()
     barrier = pltpu.get_barrier_semaphore()
     greeted = [device(*other(step)) for step in OTHERS] + list(near.values())
     greeted += [following, {"section": lax.rem(section + 7, 8)}]
     for target in greeted:
         pl.semaphore_signal(barrier, inc=1, device_id=target, device_id_type=MESH)
-    pl.semaphore_wait(barrier, len(greeted))
+
+    @pl.when(section > 4)
+    def _():
+        pl.semaphore_signal(barrier, inc=1, device_id={"section": 3}, device_id_type=MESH)
+
+    @pl.when(section == 4)
+    def _():
+        pl.semaphore_signal(barrier, inc=1, device_id={"section": 6}, device_id_type=MESH)
+
+    extra = jnp.where(section == 3, 3, jnp.where(section == 6, 1, 0))
+    pl.semaphore_wait(barrier, len(greeted) + extra)
 
     mine = head_slice(hi, x, lo)
     source = {Q: q, K: k, V: v, CK: ck, CV: cv}
@@ -74,14 +91,21 @@
     def columns(which, head):
         return pl.ds(pl.multiple_of(which * 2 * HD + head * HD, HD), HD)
 
-    def spread(part, head):
+    def spread(part, head, sub=None):
         buffer, first = home[part]
-        landing = buffer.at[head, pl.ds(pl.multiple_of(first + seq * rows, rows), rows)]
-        piece = seq // (8 // PIECES)
+        if sub is None:
+            taken, count, piece = 0, rows, seq // (8 // PIECES)
+            place_there = first + seq * rows
+        else:
+            taken, count, piece = sub * TILE, TILE, sub
+            place_there = first + sub * block + seq * TILE
+        landing = buffer.at[head, pl.ds(pl.multiple_of(place_there, TILE), count)]
         for step in OTHERS:
             there = other(step)
             pltpu.make_async_remote_copy(
-                src_ref=source[part].at[:, columns(head_slice(there[0], there[2], there[3]), head)],
+                src_ref=source[part].at[
+                    pl.ds(taken, count), columns(head_slice(there[0], there[2], there[3]), head)
+                ],
                 dst_ref=landing,
                 send_sem=sends.at[part, head],
                 recv_sem=arrivals.at[part, head, piece],
@@ -89,7 +113,7 @@
                 device_id_type=MESH,
             ).start()
         pltpu.make_async_copy(
-            source[part].at[:, columns(mine, head)], landing, arrivals.at[part, head, piece]
+            source[part].at[pl.ds(taken, count), columns(mine, head)], landing, arrivals.at[part, head, piece]
         ).start()
 
     def shift():
@@ -102,22 +126,75 @@
             device_id_type=MESH,
         )
 
+    quarter = rows // 4
+
+    def detour(number):
+        taken = resid.at[pl.ds(number * quarter, quarter)]
+        return pltpu.make_async_remote_copy(
+            src_ref=taken,
+            dst_ref=inc.at[pl.ds(0, quarter)] if number == 0 else via,
+            send_sem=shifts.at[0],
+            recv_sem=shifts.at[1] if number == 0 else detours.at[0],
+            device_id={"section": 4 + number},
+            device_id_type=MESH,
+        )
+
+    def forward(number):
+        return pltpu.make_async_remote_copy(
+            src_ref=via,
+            dst_ref=inc.at[pl.ds(number * quarter, quarter)],
+            send_sem=detours.at[1],
+            recv_sem=shifts.at[1],
+            device_id={"section": 4},
+            device_id_type=MESH,
+        )
+
+    def send_resid():
+        @pl.when(jnp.logical_and(section < 7, section != 3))
+        def _():
+            shift().start()
+
+    def send_detours():
+        @pl.when(section == 3)
+        def _():
+            for number in range(4):
+                detour(number).start()
+
+    def forward_detours():
+        for number in range(1, 4):
+
+            @pl.when(section == 4 + number)
+            def _():
+                settle(via, detours.at[0])
+                forward(number).start()
+
     is_last = section == 7
 
     @pl.when(is_last)
     def _():
-        for part, head in ((K, 0), (V, 0), (K, 1), (V, 1), (Q, 0), (CK, 0), (CV, 0), (Q, 1), (CK, 1), (CV, 1)):
+        for part, head in ((K, 0), (V, 0), (K, 1), (V, 1), (Q, 0), (Q, 1)):
             spread(part, head)
 
     @pl.when(jnp.logical_not(is_last))
     def _():
         for head in range(2):
-            for part in (K, V, Q, CK, CV):
+            for part in (K, V, Q):
                 spread(part, head)
 
-    @pl.when(jnp.logical_and(section < 7, section != 3))
-    def _():
-        shift().start()
+    def fill(tile, carry):
+        lanes = [jnp.full((1, TILE), mask[u, tile], jnp.int32) for u in range(span // TILE)]
+        bias[tile] = jnp.where(jnp.concatenate(lanes, axis=1) > 0, 0.0, LOW)
+        return carry
+
+    lax.fori_loop(0, 3 * span // TILE, fill, 0)
+    for copy, held, picked in zip(caches, (all_ck, all_cv), (ck, cv)):
+        copy.wait()
+        for i in range(4):
+            picked[pl.ds(i * quarter, quarter), :] = held[chosen[0], pl.ds(i * quarter, quarter), :]
+
+    @pl.when(section == 0)
+    def _():
+        inc[...] = jnp.zeros_like(inc)
 
     top[...] = jnp.full_like(top, LOW / 2)
     total[...] = jnp.zeros_like(total)
@@ -129,6 +206,10 @@
     def arrived(part, head, piece):
         buffer, first = home[part]
         settle(buffer.at[head, pl.ds(first + piece * part_rows, part_rows)], arrivals.at[part, head, piece])
+
+    def cached_arrived(part, head, sub):
+        buffer, first = home[part]
+        settle(buffer.at[head, pl.ds(first + sub * block, block)], arrivals.at[part, head, sub])
 
     def all_arrived(part, head):
         for piece in range(PIECES):
@@ -151,9 +232,9 @@
             device_id_type=MESH,
         )
 
-    def relay(tree, head, piece):
+    def relay(tree, head, piece, nodes=(0, 3, 4, 5, 6)):
         for node, targets in TREES[tree].items():
-            if node == 7:
+            if node not in nodes:
                 continue
 
             @pl.when(section == node)
@@ -185,44 +266,51 @@
     @pl.when(jnp.logical_not(is_last))
     def _():
         for piece in range(PIECES):
-            relay(0, 0, piece)
+            relay(0, 0, piece, NEARER)
         all_arrived(K, 0)
         all_arrived(Q, 0)
 
+    for head in range(2):
+        for sub in range(2):
+            for part in (CK, CV):
+                spread(part, head, sub)
+
     def do(action, *args):
         return functools.partial(action, *args)
 
+    late = {
+        (5, 0): [send_resid],
+        (7, 0): [send_detours],
+        (7, 1): [do(cached_arrived, CK, 0, 0)],
+        (8, 0): [do(cached_arrived, CV, 0, 0)],
+        (8, 1): [do(cached_arrived, CK, 0, 1)],
+        (9, 0): [do(cached_arrived, CV, 0, 1)],
+        (9, 1): [do(cached_arrived, CK, 1, 0)],
+        (10, 0): [do(cached_arrived, CV, 1, 0)],
+        (10, 1): [do(cached_arrived, CK, 1, 1)],
+        (11, 0): [do(cached_arrived, CV, 1, 1), forward_detours],
+    }
     others = {
         (0, 0): [do(all_arrived, V, 0), do(relay, 1, 0, 0)],
-        (0, 1): [do(relay, 1, 0, 1)],
-        (1, 0): [do(relay, 1, 0, 2)],
-        (1, 1): [do(relay, 1, 0, 3)] + [do(relay, 0, 1, p) for p in range(4)] + [do(all_arrived, CK, 0)],
-        (2, 0): [do(all_arrived, CV, 0), do(relay, 1, 1, 0)],
-        (2, 1): [do(relay, 1, 1, 1)],
-        (3, 0): [do(relay, 1, 1, 2)],
-        (3, 1): [do(relay, 1, 1, 3), do(take_fresh, 0, 0, (0, 1))],
-        (4, 0): [do(take_fresh, 1, 0, (0, 1))],
-        (4, 1): [do(take_fresh, 0, 0, (2, 3))],
-        (5, 0): [do(take_fresh, 1, 0, (2, 3))],
-        (5, 1): [do(all_arrived, Q, 1), do(all_arrived, K, 1)],
-        (6, 0): [do(all_arrived, V, 1)],
-        (7, 1): [do(take_fresh, 0, 1, (0, 1))],
-        (8, 0): [do(take_fresh, 1, 1, (0, 1))],
-        (8, 1): [do(take_fresh, 0, 1, (2, 3))],
-        (9, 0): [do(take_fresh, 1, 1, (2, 3))],
-        (9, 1): [do(all_arrived, CK, 1)],
-        (10, 0): [do(all_arrived, CV, 1)],
+        (0, 1): [do(relay, 1, 0, 1), do(relay, 0, 0, 0, (3,))],
+        (1, 0): [do(relay, 1, 0, 2), do(relay, 0, 0, 1, (3,))],
+        (1, 1): [do(relay, 1, 0, 3), do(relay, 0, 0, 2, (3,)), do(relay, 0, 0, 3, (3,))]
+        + [do(relay, 0, 1, p, NEARER) for p in range(4)]
+        + [do(take_fresh, 0, 0, (0, 1))],
+        (2, 0): [do(take_fresh, 1, 0, (0, 1)), do(relay, 1, 1, 0), do(relay, 0, 1, 0, (3,))],
+        (2, 1): [do(take_fresh, 0, 0, (2, 3)), do(relay, 1, 1, 1), do(relay, 0, 1, 1, (3,))],
+        (3, 0): [do(take_fresh, 1, 0, (2, 3)), do(relay, 1, 1, 2), do(relay, 0, 1, 2, (3,))],
+        (3, 1): [do(relay, 1, 1, 3), do(relay, 0, 1, 3, (3,)), do(all_arrived, Q, 1), do(all_arrived, K, 1)],
+        (4, 0): [do(all_arrived, V, 1)],
+        (5, 1): [do(take_fresh, 0, 1, (0, 1))],
+        (6, 0): [do(take_fresh, 1, 1, (0, 1))],
+        (6, 1): [do(take_fresh, 0, 1, (2, 3))],
+        (7, 0): [do(take_fresh, 1, 1, (2, 3))],
     }
-    last = {
-        (3, 1): [do(all_arrived, CK, 0)],
-        (4, 0): [do(all_arrived, CV, 0)],
-        (5, 1): [do(all_arrived, Q, 1)],
-        (9, 1): [do(all_arrived, CK, 1)],
-        (10, 0): [do(all_arrived, CV, 1)],
-    }
+    last = {(3, 1): [do(all_arrived, Q, 1)]}
 
     def point(stage, at):
-        for wanted, table in ((is_last, last), (jnp.logical_not(is_last), others)):
+        for wanted, table in ((is_last, last), (jnp.logical_not(is_last), others), (section >= 0, late)):
             for (number, where), actions in table.items():
                 if where == at:
 
@@ -234,12 +322,14 @@
     tiles = block // TILE
 
     def locate(stage):
-        head, step = stage // 6, lax.rem(stage, 6)
-        move = jnp.where(step < 2, 0, jnp.where(step < 4, 2, -2))
-        index = step + jnp.where(jnp.logical_or(is_last, head == 1), 0, move)
-        fresh_block = jnp.logical_and(index >= 2, index < 4)
-        stored = index - jnp.where(jnp.logical_and(is_last, fresh_block), 2, 0)
-        return head, index, pl.ds(pl.multiple_of(stored * block, block), block)
+        pair = stage // 2
+        cached = pair >= 4
+        head = jnp.where(cached, pair - 4, pair // 2)
+        kind = jnp.where(cached, 2, lax.rem(pair, 2))
+        index = 2 * kind + lax.rem(stage, 2)
+        stored = index - jnp.where(jnp.logical_and(is_last, kind == 1), 2, 0)
+        first = jnp.where(cached, 4 * tiles + lax.rem(stage, 2), index * tiles)
+        return head, (first, jnp.where(cached, 2, 1)), pl.ds(pl.multiple_of(stored * block, block), block)
 
     def half_rows(half):
         return pl.ds(pl.multiple_of(half * block, block), block)
@@ -254,14 +344,8 @@
         )
 
     def absorb(stage, half, scores):
-        head, index, keys = locate(stage)
-        biases = [
-            jnp.concatenate(
-                [jnp.full((1, TILE), bias[half * tiles + u, index * tiles + t], F32) for u in range(tiles)],
-                axis=1,
-            )
-            for t in range(tiles)
-        ]
+        head, (first, pace), keys = locate(stage)
+        biases = [bias[first + t * pace, :, half_rows(half)] for t in range(tiles)]
         old = top[head, half]
         new = old
         for t in range(tiles):
@@ -310,13 +394,8 @@
     score(0, far, score_a)
 
     def stage_body(stage, carry):
-        head, ends = stage // 6, lax.rem(stage, 6) == 5
+        head, ends = stage // 11, jnp.logical_or(stage == 9, stage == 11)
         point(stage, 0)
-
-        @pl.when(jnp.logical_and(stage == 6, section == 3))
-        def _():
-            shift().start()
-
         score(stage, 1 - far, score_b)
         absorb(stage, far, score_a)
 
@@ -348,29 +427,35 @@
 
     @pl.when(section < 7)
     def _():
-        shift().wait_send()
+        settle(resid, shifts.at[0])
+
+    @pl.when(section > 4)
+    def _():
+        settle(via, detours.at[1])
 
     @pl.when(section > 0)
     def _():
-        shift().wait_recv()
+        settle(inc, shifts.at[1])
 
     for head in range(2):
         for part in range(5):
             settle(home[part][0].at[head, pl.ds(0, 7 * rows)], sends.at[part, head])
         settle(ob.at[head, pl.ds(0, 7 * rows)], out_sends.at[head])
         settle(ob.at[head], out_arrivals.at[head])
-
-
-def fused(q, k, v, ck, cv, resid, bias):
+    out[...] = (inc[...].astype(F32) + attn[...].astype(F32)).astype(BF16)
+
+
+def fused(q, k, v, cache_k, cache_v, resid, chosen, mask):
     rows, width = q.shape
     span = rows * 8
     half = span // 2
     dma = pltpu.SemaphoreType.DMA
+    smem = pl.BlockSpec(memory_space=pltpu.SMEM)
     return pl.pallas_call(
         functools.partial(fused_kernel, span),
-        out_shape=(jax.ShapeDtypeStruct((rows, width), BF16), jax.ShapeDtypeStruct((rows, width), BF16)),
-        in_specs=[HBM] * 6 + [pl.BlockSpec(memory_space=pltpu.SMEM)],
-        out_specs=[HBM] * 2,
+        out_shape=jax.ShapeDtypeStruct((rows, width), BF16),
+        in_specs=[HBM] * 6 + [smem] * 2,
+        out_specs=VMEM,
         scratch_shapes=[
             pltpu.VMEM((2, span, HD), BF16),
             pltpu.VMEM((2, 3 * span, HD), BF16),
@@ -381,6 +466,14 @@
             pltpu.VMEM((2, 2, 1, half), F32),
             pltpu.VMEM((2, 2, 1, half), F32),
             pltpu.VMEM((2, 2, HD, half), F32),
+            pltpu.VMEM((3 * span // TILE, 1, span), F32),
+            pltpu.VMEM(cache_k.shape, BF16),
+            pltpu.VMEM(cache_v.shape, BF16),
+            pltpu.VMEM((rows, width), BF16),
+            pltpu.VMEM((rows, width), BF16),
+            pltpu.VMEM((rows, width), BF16),
+            pltpu.VMEM((rows, width), BF16),
+            pltpu.VMEM((rows // 4, width), BF16),
             dma((5, 2)),
             dma((5, 2, PIECES)),
             dma((2,)),
@@ -388,21 +481,20 @@
             dma((2, 2, PIECES, 2)),
             dma((2,)),
             dma((2,)),
+            dma((2,)),
+            dma((2,)),
         ],
         name="fused",
         compiler_params=pltpu.CompilerParams(
             collective_id=0, has_side_effects=True, vmem_limit_bytes=60 * 2**20
         ),
-    )(q, k, v, ck, cv, resid, bias)
+    )(q, k, v, cache_k, cache_v, resid, chosen, mask)
 
 
 def body(resid, span_q, span_k, span_v, cache_k, cache_v, cache_index, tile_mask):
-    cached_k = lax.dynamic_index_in_dim(cache_k, cache_index[0], 0, keepdims=False)
-    cached_v = lax.dynamic_index_in_dim(cache_v, cache_index[0], 0, keepdims=False)
-    bias = jnp.where(tile_mask[0] > 0, 0.0, LOW).astype(F32)
-    attn, incoming = fused(span_q[0], span_k[0], span_v[0], cached_k, cached_v, resid[0], bias)
-    incoming = jnp.where(lax.axis_index("section") == 0, jnp.zeros_like(incoming), incoming)
-    return (incoming.astype(F32) + attn.astype(F32)).astype(BF16)[None]
+    return fused(
+        span_q[0], span_k[0], span_v[0], cache_k, cache_v, resid[0], cache_index, tile_mask[0]
+    )[None]
 
 
 def solution(mesh):

time: 116 us -> 95.1 us (0.82)
  Pallas kernels: 109 us -> 91.5 us
  other arithmetic: 3.19 us -> 0 us
    pallas_call x1, Pallas kernels: 109 us -> 91.5 us  [fused(): pl.pallas_call(functools.partial(fused_kernel, span), out_shape=jax.Shape...]
    squeeze x1 -> x0, local copies, waits for them, and re-layouts: 3.11 us -> none  [body(): lax.dynamic_index_in_dim(cache_v, cache_index[0], 0, keepdims=False)]
    broadcast_in_dim x1 -> x0, other arithmetic: 2.59 us -> none  [body(): return (incoming.astype(F32) + attn.astype(F32)).astype(BF16)[None]]
    unnamed x2 -> x1, local copies, waits for them, and re-layouts: 0.01 us -> 2.3 us
where the time goes in v2:
time: 95.1 us; the launch traced here: 94.5 us
  Pallas kernels  91.5 us (96%)
  local copies, waits for them, and re-layouts  2.3 us (2%)
    pallas_call x1, Pallas kernels, fused(): pl.pallas_call(functools.partial(fused_kernel, span), out_shape=jax.Shape...  91.5 us
    unnamed x1, local copies, waits for them, and re-layouts  2.3 us

profile of v2, /device:TPU:0, one launch (start us, length us, event | category | flops | bytes accessed | tf_op | source)
XLA Modules:
  0.0 94.5 jit_solution(13826833308029459951)
XLA Ops:
  0.7 91.5 %fused.1 = bf16[256,2048]{1,0:T(8,128)(2,1)} custom-call(bf16[256,2048]{1,0:T(8,128)(2,1)} %bitcast.7, bf16[256,2048]{1,0:T(8,128)(2,1)} %bitcast.8, bf16[256,2048]{1,0:T(8,128)(2,1)} %bitcast.9, bf16[4,256,2048]{2,1,0:T(8,128)(2,1)} %cache_k.1, bf16[4,256,2048]{2,1,0:T(8,128)(2,1)} %cache_v.1, bf16[256,2048]{1,0:T(8,128)(2,1)} %bitcast.10, ...), custom_call_target="tpu_custom_call" | custom-call | tf_op jit(solution)/shard_map/fused/pallas_call | solution.py:454
  92.2 2.3 %copy.11 = bf16[1,256,2048]{2,1,0:T(8,128)(2,1)} copy(bf16[1,256,2048]{2,1,0:T(8,128)(2,1)} %bitcast.6) | data formatting | bytes 2097152

commit v3 on v2

--- a/solution.py
+++ b/solution.py
@@ -42,7 +42,7 @@
     {7: ("down", "cross"), 6: ("down", "cross"), 3: ("up",), 5: ("down", "cross")},
 )
 PIECES = 4
-NEARER = (4, 5, 0)
+EARLY = 3
 LOW = -1e30
 Q, K, V, CK, CV = range(5)
 
@@ -116,10 +116,11 @@
             source[part].at[pl.ds(taken, count), columns(mine, head)], landing, arrivals.at[part, head, piece]
         ).start()
 
-    def shift():
+    def shift(number):
+        strip = pl.ds(number * (rows // 8), rows // 8)
         return pltpu.make_async_remote_copy(
-            src_ref=resid,
-            dst_ref=inc,
+            src_ref=resid.at[strip],
+            dst_ref=inc.at[strip],
             send_sem=shifts.at[0],
             recv_sem=shifts.at[1],
             device_id=following,
@@ -149,16 +150,18 @@
             device_id_type=MESH,
         )
 
-    def send_resid():
-        @pl.when(jnp.logical_and(section < 7, section != 3))
-        def _():
-            shift().start()
-
-    def send_detours():
+    shared = functools.reduce(jnp.logical_or, [section == node for node in (0, 4, 5)])
+
+    def send_resid(numbers, where):
+        @pl.when(jnp.logical_and(where, jnp.logical_and(section < 7, section != 3)))
+        def _():
+            for number in numbers:
+                shift(number).start()
+
+    def send_detour(number):
         @pl.when(section == 3)
         def _():
-            for number in range(4):
-                detour(number).start()
+            detour(number).start()
 
     def forward_detours():
         for number in range(1, 4):
@@ -170,20 +173,31 @@
 
     is_last = section == 7
 
+    send_resid(range(EARLY), section >= 0)
+
     @pl.when(is_last)
     def _():
-        for part, head in ((K, 0), (V, 0), (K, 1), (V, 1), (Q, 0), (Q, 1)):
+        for part, head in ((K, 0), (V, 0), (K, 1)):
             spread(part, head)
 
     @pl.when(jnp.logical_not(is_last))
     def _():
-        for head in range(2):
-            for part in (K, V, Q):
-                spread(part, head)
+        for part in (K, V, Q):
+            spread(part, 0)
+
+    send_resid(range(EARLY, 8), jnp.logical_not(shared))
 
     def fill(tile, carry):
         lanes = [jnp.full((1, TILE), mask[u, tile], jnp.int32) for u in range(span // TILE)]
-        bias[tile] = jnp.where(jnp.concatenate(lanes, axis=1) > 0, 0.0, LOW)
+        allowed = jnp.concatenate(lanes, axis=1)
+        bias[tile] = jnp.where(allowed > 0, 0.0, LOW)
+
+        @pl.when(jnp.logical_and(is_last, tile < span // TILE))
+        def _():
+            again = [jnp.full((1, TILE), mask[u, tile + span // TILE], jnp.int32) for u in range(span // TILE)]
+            times = allowed + jnp.concatenate(again, axis=1)
+            bias[tile] = jnp.where(times > 1, 1.0 / RATE, jnp.where(times > 0, 0.0, LOW))
+
         return carry
 
     lax.fori_loop(0, 3 * span // TILE, fill, 0)
@@ -191,6 +205,10 @@
         copy.wait()
         for i in range(4):
             picked[pl.ds(i * quarter, quarter), :] = held[chosen[0], pl.ds(i * quarter, quarter), :]
+
+    def spread_cached(part, head):
+        for sub in range(2):
+            spread(part, head, sub)
 
     @pl.when(section == 0)
     def _():
@@ -253,64 +271,109 @@
             for piece in pieces:
                 fresh_arrived(tree, head, piece)
 
+    def do(action, *args):
+        return functools.partial(action, *args)
+
     @pl.when(is_last)
     def _():
+        following_sends = iter((do(spread, V, 1), do(spread, Q, 0), do(spread, Q, 1), do(spread_cached, CK, 0)))
         for head in range(2):
             for tree, part in ((0, K), (1, V)):
                 for piece in range(PIECES):
                     arrived(part, head, piece)
                     for slot, target in enumerate(TREES[tree][7]):
                         pass_on(tree, head, piece, 0, slot, target).start()
+                next(following_sends)()
         all_arrived(Q, 0)
+        spread_cached(CV, 0)
 
     @pl.when(jnp.logical_not(is_last))
     def _():
-        for piece in range(PIECES):
-            relay(0, 0, piece, NEARER)
         all_arrived(K, 0)
+        spread_cached(CK, 0)
+        for piece in range(2):
+            relay(0, 0, piece, (4,))
+        all_arrived(V, 0)
+        spread_cached(CV, 0)
+        for piece in range(2, 4):
+            relay(0, 0, piece, (4,))
         all_arrived(Q, 0)
-
-    for head in range(2):
-        for sub in range(2):
-            for part in (CK, CV):
-                spread(part, head, sub)
-
-    def do(action, *args):
-        return functools.partial(action, *args)
-
-    late = {
-        (5, 0): [send_resid],
-        (7, 0): [send_detours],
-        (7, 1): [do(cached_arrived, CK, 0, 0)],
-        (8, 0): [do(cached_arrived, CV, 0, 0)],
-        (8, 1): [do(cached_arrived, CK, 0, 1)],
-        (9, 0): [do(cached_arrived, CV, 0, 1)],
-        (9, 1): [do(cached_arrived, CK, 1, 0)],
-        (10, 0): [do(cached_arrived, CV, 1, 0)],
-        (10, 1): [do(cached_arrived, CK, 1, 1)],
-        (11, 0): [do(cached_arrived, CV, 1, 1), forward_detours],
+        spread(Q, 1)
+
+    def tail(first):
+        return {
+            (first - 1, 1): [do(cached_arrived, CK, 1, 0)],
+            (first, 0): [do(cached_arrived, CV, 1, 0)],
+            (first, 1): [do(cached_arrived, CK, 1, 1)],
+            (first + 1, 0): [do(cached_arrived, CV, 1, 1), forward_detours],
+        }
+
+    others = {
+        (0, 0): [do(relay, 1, 0, 0), do(relay, 0, 0, 0, (0, 5))],
+        (0, 1): [do(relay, 1, 0, 1), do(relay, 0, 0, 1, (0, 5))],
+        (1, 0): [do(relay, 1, 0, 2), do(relay, 0, 0, 2, (0, 5)), do(relay, 0, 0, 0, (3,))],
+        (1, 1): [do(relay, 1, 0, 3), do(relay, 0, 0, 3, (0, 5))]
+        + [do(relay, 0, 0, p, (3,)) for p in (1, 2, 3)]
+        + [do(relay, 0, 1, p, (4,)) for p in range(4)]
+        + [do(cached_arrived, CK, 0, 0), do(spread, K, 1)],
+        (2, 0): [do(cached_arrived, CV, 0, 0), do(relay, 1, 1, 0, (6, 3)), do(relay, 0, 1, 0, (0, 5))],
+        (2, 1): [
+            do(spread, V, 1),
+            do(cached_arrived, CK, 0, 1),
+            do(relay, 1, 1, 1, (6, 3)),
+            do(relay, 0, 1, 1, (0, 5)),
+        ],
+        (3, 0): [
+            do(cached_arrived, CV, 0, 1),
+            do(relay, 1, 1, 2, (6, 3)),
+            do(relay, 0, 1, 2, (0, 5)),
+            do(relay, 1, 1, 0, (5,)),
+            do(relay, 0, 1, 0, (3,)),
+        ],
+        (3, 1): [
+            do(spread_cached, CK, 1),
+            do(send_resid, (3, 4), shared),
+            do(relay, 1, 1, 3, (6, 3)),
+            do(relay, 0, 1, 3, (0, 5)),
+            do(relay, 1, 1, 1, (5,)),
+            do(relay, 0, 1, 1, (3,)),
+            do(take_fresh, 0, 0, (0, 1)),
+        ],
+        (4, 0): [
+            do(send_resid, (5,), shared),
+            do(take_fresh, 1, 0, (0, 1)),
+            do(relay, 1, 1, 2, (5,)),
+            do(relay, 0, 1, 2, (3,)),
+        ],
+        (4, 1): [
+            do(take_fresh, 0, 0, (2, 3)),
+            do(relay, 1, 1, 3, (5,)),
+            do(relay, 0, 1, 3, (3,)),
+            do(spread_cached, CV, 1),
+            do(send_resid, (6, 7), shared),
+        ],
+        (5, 0): [do(take_fresh, 1, 0, (2, 3))],
+        (5, 1): [do(all_arrived, Q, 1), do(take_fresh, 0, 1, (0, 1))],
+        (6, 0): [do(send_detour, 1), do(take_fresh, 1, 1, (0, 1))],
+        (6, 1): [do(take_fresh, 0, 1, (2, 3))],
+        (7, 0): [do(send_detour, 2), do(take_fresh, 1, 1, (2, 3))],
+        (7, 1): [do(all_arrived, K, 1)],
+        (8, 0): [do(send_detour, 3), do(all_arrived, V, 1)],
+        (9, 0): [do(send_detour, 0)],
+        **tail(10),
     }
-    others = {
-        (0, 0): [do(all_arrived, V, 0), do(relay, 1, 0, 0)],
-        (0, 1): [do(relay, 1, 0, 1), do(relay, 0, 0, 0, (3,))],
-        (1, 0): [do(relay, 1, 0, 2), do(relay, 0, 0, 1, (3,))],
-        (1, 1): [do(relay, 1, 0, 3), do(relay, 0, 0, 2, (3,)), do(relay, 0, 0, 3, (3,))]
-        + [do(relay, 0, 1, p, NEARER) for p in range(4)]
-        + [do(take_fresh, 0, 0, (0, 1))],
-        (2, 0): [do(take_fresh, 1, 0, (0, 1)), do(relay, 1, 1, 0), do(relay, 0, 1, 0, (3,))],
-        (2, 1): [do(take_fresh, 0, 0, (2, 3)), do(relay, 1, 1, 1), do(relay, 0, 1, 1, (3,))],
-        (3, 0): [do(take_fresh, 1, 0, (2, 3)), do(relay, 1, 1, 2), do(relay, 0, 1, 2, (3,))],
-        (3, 1): [do(relay, 1, 1, 3), do(relay, 0, 1, 3, (3,)), do(all_arrived, Q, 1), do(all_arrived, K, 1)],
-        (4, 0): [do(all_arrived, V, 1)],
-        (5, 1): [do(take_fresh, 0, 1, (0, 1))],
-        (6, 0): [do(take_fresh, 1, 1, (0, 1))],
-        (6, 1): [do(take_fresh, 0, 1, (2, 3))],
-        (7, 0): [do(take_fresh, 1, 1, (2, 3))],
+    last = {
+        (1, 1): [do(all_arrived, Q, 1), do(spread_cached, CK, 1)],
+        (2, 1): [do(spread_cached, CV, 1)],
+        (3, 1): [do(cached_arrived, CK, 0, 0)],
+        (4, 0): [do(cached_arrived, CV, 0, 0)],
+        (4, 1): [do(cached_arrived, CK, 0, 1)],
+        (5, 0): [do(cached_arrived, CV, 0, 1)],
+        **tail(6),
     }
-    last = {(3, 1): [do(all_arrived, Q, 1)]}
 
     def point(stage, at):
-        for wanted, table in ((is_last, last), (jnp.logical_not(is_last), others), (section >= 0, late)):
+        for wanted, table in ((is_last, last), (jnp.logical_not(is_last), others)):
             for (number, where), actions in table.items():
                 if where == at:
 
@@ -323,13 +386,13 @@
 
     def locate(stage):
         pair = stage // 2
-        cached = pair >= 4
-        head = jnp.where(cached, pair - 4, pair // 2)
-        kind = jnp.where(cached, 2, lax.rem(pair, 2))
+        head = jnp.where(is_last, lax.rem(pair, 2), pair // 3)
+        kind_others = jnp.where(pair < 3, lax.rem(2 * pair, 3), lax.rem(2 * pair + 1, 3))
+        kind = jnp.where(is_last, 2 * (pair // 2), kind_others)
+        cached = kind == 2
         index = 2 * kind + lax.rem(stage, 2)
-        stored = index - jnp.where(jnp.logical_and(is_last, kind == 1), 2, 0)
         first = jnp.where(cached, 4 * tiles + lax.rem(stage, 2), index * tiles)
-        return head, (first, jnp.where(cached, 2, 1)), pl.ds(pl.multiple_of(stored * block, block), block)
+        return head, (first, jnp.where(cached, 2, 1)), pl.ds(pl.multiple_of(index * block, block), block)
 
     def half_rows(half):
         return pl.ds(pl.multiple_of(half * block, block), block)
@@ -391,10 +454,12 @@
             ).start()
 
     far = 1 - x // 2
+    stages = jnp.where(is_last, 8, 12)
     score(0, far, score_a)
 
     def stage_body(stage, carry):
-        head, ends = stage // 11, jnp.logical_or(stage == 9, stage == 11)
+        head = stage // (stages - 1)
+        ends = jnp.logical_or(stage == 5, stage == stages - 1)
         point(stage, 0)
         score(stage, 1 - far, score_b)
         absorb(stage, far, score_a)
@@ -404,7 +469,7 @@
             finish(head, far)
 
         point(stage, 1)
-        score(jnp.minimum(stage + 1, 11), far, score_a)
+        score(jnp.minimum(stage + 1, stages - 1), far, score_a)
         absorb(stage, 1 - far, score_b)
 
         @pl.when(ends)
@@ -413,7 +478,7 @@
 
         return carry
 
-    lax.fori_loop(0, 12, stage_body, 0)
+    lax.fori_loop(0, stages, stage_body, 0)
 
     for tree in range(2):
         for node, targets in TREES[tree].items():

time: 95.1 us -> 93.2 us (0.980)
  Pallas kernels: 91.5 us -> 90 us
    pallas_call x1, Pallas kernels: 91.5 us -> 90 us  [fused(): pl.pallas_call(functools.partial(fused_kernel, span), out_shape=jax.Shape...]
where the time goes in v3:
time: 93.2 us; the launch traced here: 93 us
  Pallas kernels  90 us (97%)
  local copies, waits for them, and re-layouts  2.3 us (2%)
    pallas_call x1, Pallas kernels, fused(): pl.pallas_call(functools.partial(fused_kernel, span), out_shape=jax.Shape...  90 us
    unnamed x1, local copies, waits for them, and re-layouts  2.3 us

profile of v3, /device:TPU:0, one launch (start us, length us, event | category | flops | bytes accessed | tf_op | source)
XLA Modules:
  0.0 93.0 jit_solution(7471308905960509350)
XLA Ops:
  0.7 90.0 %fused.1 = bf16[256,2048]{1,0:T(8,128)(2,1)} custom-call(bf16[256,2048]{1,0:T(8,128)(2,1)} %bitcast.7, bf16[256,2048]{1,0:T(8,128)(2,1)} %bitcast.8, bf16[256,2048]{1,0:T(8,128)(2,1)} %bitcast.9, bf16[4,256,2048]{2,1,0:T(8,128)(2,1)} %cache_k.1, bf16[4,256,2048]{2,1,0:T(8,128)(2,1)} %cache_v.1, bf16[256,2048]{1,0:T(8,128)(2,1)} %bitcast.10, ...), custom_call_target="tpu_custom_call" | custom-call | tf_op jit(solution)/shard_map/fused/pallas_call | solution.py:519
  90.7 2.3 %copy.11 = bf16[1,256,2048]{2,1,0:T(8,128)(2,1)} copy(bf16[1,256,2048]{2,1,0:T(8,128)(2,1)} %bitcast.6) | data formatting | bytes 2097152

commit v4 on v3

--- a/solution.py
+++ b/solution.py
@@ -129,11 +129,20 @@
 
     quarter = rows // 4
 
+    starts, sizes = ((0, 1, 3, 6), (1, 2, 3, 2))
+    eighth = rows // 8
+
+    def strip_of(number):
+        return pl.ds(starts[number] * eighth, sizes[number] * eighth)
+
+    def carried(number):
+        return via.at[pl.ds(0, sizes[number] * eighth)]
+
     def detour(number):
-        taken = resid.at[pl.ds(number * quarter, quarter)]
+        taken = resid.at[strip_of(number)]
         return pltpu.make_async_remote_copy(
             src_ref=taken,
-            dst_ref=inc.at[pl.ds(0, quarter)] if number == 0 else via,
+            dst_ref=inc.at[strip_of(0)] if number == 0 else carried(number),
             send_sem=shifts.at[0],
             recv_sem=shifts.at[1] if number == 0 else detours.at[0],
             device_id={"section": 4 + number},
@@ -142,8 +151,8 @@
 
     def forward(number):
         return pltpu.make_async_remote_copy(
-            src_ref=via,
-            dst_ref=inc.at[pl.ds(number * quarter, quarter)],
+            src_ref=carried(number),
+            dst_ref=inc.at[strip_of(number)],
             send_sem=detours.at[1],
             recv_sem=shifts.at[1],
             device_id={"section": 4},
@@ -168,7 +177,7 @@
 
             @pl.when(section == 4 + number)
             def _():
-                settle(via, detours.at[0])
+                settle(carried(number), detours.at[0])
                 forward(number).start()
 
     is_last = section == 7
@@ -494,9 +503,11 @@
     def _():
         settle(resid, shifts.at[0])
 
-    @pl.when(section > 4)
-    def _():
-        settle(via, detours.at[1])
+    for number in range(1, 4):
+
+        @pl.when(section == 4 + number)
+        def _():
+            settle(carried(number), detours.at[1])
 
     @pl.when(section > 0)
     def _():
@@ -538,7 +549,7 @@
             pltpu.VMEM((rows, width), BF16),
             pltpu.VMEM((rows, width), BF16),
             pltpu.VMEM((rows, width), BF16),
-            pltpu.VMEM((rows // 4, width), BF16),
+            pltpu.VMEM((3 * rows // 8, width), BF16),
             dma((5, 2)),
             dma((5, 2, PIECES)),
             dma((2,)),

time: 93.2 us -> 97.5 us (1.046)
  the two profiles are of different devices: /device:TPU:0 before, /device:TPU:68 now
where the time goes in v4:
time: 97.5 us; the launch traced here: 97.3 us
  Pallas kernels  94.3 us (97%)
  local copies, waits for them, and re-layouts  2.3 us (2%)
    pallas_call x1, Pallas kernels, fused(): pl.pallas_call(functools.partial(fused_kernel, span), out_shape=jax.Shape...  94.3 us
    unnamed x1, local copies, waits for them, and re-layouts  2.3 us

profile of v4, /device:TPU:68, one launch (start us, length us, event | category | flops | bytes accessed | tf_op | source)
XLA Modules:
  0.0 97.3 jit_solution(8380493556653709994)
XLA Ops:
  0.7 94.3 %fused.1 = bf16[256,2048]{1,0:T(8,128)(2,1)} custom-call(bf16[256,2048]{1,0:T(8,128)(2,1)} %bitcast.7, bf16[256,2048]{1,0:T(8,128)(2,1)} %bitcast.8, bf16[256,2048]{1,0:T(8,128)(2,1)} %bitcast.9, bf16[4,256,2048]{2,1,0:T(8,128)(2,1)} %cache_k.1, bf16[4,256,2048]{2,1,0:T(8,128)(2,1)} %cache_v.1, bf16[256,2048]{1,0:T(8,128)(2,1)} %bitcast.10, ...), custom_call_target="tpu_custom_call" | custom-call | tf_op jit(solution)/shard_map/fused/pallas_call | solution.py:530
  95.0 2.3 %copy.11 = bf16[1,256,2048]{2,1,0:T(8,128)(2,1)} copy(bf16[1,256,2048]{2,1,0:T(8,128)(2,1)} %bitcast.6) | data formatting | bytes 2097152
